TPU v7x, 256 devices: a whole 4x4x8 slice. The times are simulated.
256 devices in a mesh: outer: 8 (over x_hi, y), inner: 32 (over x_lo, z, core).
Axes of the slice: x: 4 (x_hi: 2, x_lo: 2; x = x_hi * 2 + x_lo), y: 4, z: 8, core: 2. Of those that a mesh axis runs over, the one named last changes fastest.
Arguments:
- vectors: bfloat16 [524288, 256], P(('outer', 'inner')), may hold values from -6 to 6
- leaf_basis: bfloat16 [524288, 256], P(('outer', 'inner')), may hold values from -0.375 to 0.375
- transfer: bfloat16 [4, 8, 32, 8, 512, 256], P(None, 'outer', 'inner'), may hold values from -0.25 to 0.25
- core_mats: bfloat16 [8, 32, 8, 256, 256], P('outer', 'inner'), may hold values from -0.375 to 0.375
- row_basis: bfloat16 [524288, 256], P(('outer', 'inner')), may hold values from -0.375 to 0.375
- box_order: int32 [8, 32, 8], P('outer', 'inner'), may hold values from 0 to 7, each once within a row
Outputs:
- applied: bfloat16 [524288, 256], P(('outer', 'inner'))
Inputs may be any that keep to these rules, and one draw needn't show every extreme that they name: `box_order`: for every device the 8 entries are a permutation of 0 to 7.
All inputs are finite; a program needn't handle non-finite values.
Results may differ from a plain program's by a relative error of at most 0.011.
Values may be sent and summed in bfloat16 or wider, within the bound.
A program may use at most 64 MiB of HBM per device.

v0:
```python
import jax
import jax.numpy as jnp
from jax import lax
from jax.sharding import PartitionSpec as P

LEVELS = 4


def swapped(array, axis, apart):
    return lax.ppermute(array, axis, [(i, i ^ 1 << apart) for i in range(lax.axis_size(axis))])


def split_half(box_state, half_flag):
    half_count = box_state.shape[0] // 2
    kept_half = lax.dynamic_slice_in_dim(box_state, half_flag * half_count, half_count, 0)
    sent_half = lax.dynamic_slice_in_dim(box_state, (1 - half_flag) * half_count, half_count, 0)
    return (kept_half, sent_half)


def merge_level(kept_half, received, half_flag, level_w):
    half_count = kept_half.shape[0]
    columns = kept_half.shape[1]
    rank_dim = kept_half.shape[2]
    paired_w = level_w.reshape(half_count, 2, 2 * rank_dim, rank_dim)
    low_part = jnp.where(half_flag == 0, kept_half, received)
    high_part = jnp.where(half_flag == 0, received, kept_half)
    stacked = jnp.concatenate([low_part, high_part], axis=2)
    merged = jnp.einsum("kcs,kosr->kocr", stacked, paired_w, preferred_element_type=jnp.float32)
    return merged.reshape(2 * half_count, columns, rank_dim).astype(jnp.bfloat16)


def on_device(vectors, leaf_basis, transfer, core_mats, row_basis, box_order):
    box_count = transfer.shape[3]
    rank_dim = leaf_basis.shape[1]
    columns = vectors.shape[1]
    leaf_rows = vectors.shape[0] // box_count
    local_x = vectors.reshape(box_count, leaf_rows, columns)
    local_v = leaf_basis.reshape(box_count, leaf_rows, rank_dim)
    box_state = jnp.einsum(
        "klc,klr->kcr", local_x, local_v, preferred_element_type=jnp.float32
    ).astype(jnp.bfloat16)
    weights = transfer.reshape(transfer.shape[0], box_count, 2 * rank_dim, rank_dim)
    for level_idx in range(LEVELS):
        if level_idx < 2:
            bit_pos = level_idx
            half_flag = jnp.bitwise_and(jnp.right_shift(lax.axis_index("inner"), bit_pos), 1)
            kept_half, sent_half = split_half(box_state, half_flag)
            received = swapped(sent_half, "inner", bit_pos)
        else:
            bit_pos = level_idx - 2
            half_flag = jnp.bitwise_and(jnp.right_shift(lax.axis_index("outer"), bit_pos), 1)
            kept_half, sent_half = split_half(box_state, half_flag)
            received = swapped(sent_half, "outer", bit_pos)
        box_state = merge_level(kept_half, received, half_flag, weights[level_idx])
    slot_order = box_order.reshape(box_count)
    chosen = jnp.take(box_state, slot_order, axis=0)
    cores = core_mats.reshape(box_count, rank_dim, rank_dim)
    core_out = jnp.einsum("kcs,ksr->kcr", chosen, cores, preferred_element_type=jnp.float32).astype(
        jnp.bfloat16
    )
    inner_count = lax.axis_size("inner")
    local_u = row_basis.reshape(box_count, leaf_rows, rank_dim)
    row_out = jnp.einsum(
        "klr,kcr->klc", local_u, core_out, preferred_element_type=jnp.float32
    ).astype(jnp.bfloat16)
    pieces = row_out.reshape(inner_count, -1, columns)
    arrived = lax.all_to_all(pieces, "inner", split_axis=0, concat_axis=0, tiled=True)
    return arrived.reshape(box_count * leaf_rows, columns)


def solution(mesh):
    in_specs = (
        P(("outer", "inner"), None),
        P(("outer", "inner"), None),
        P(None, "outer", "inner", None, None, None),
        P("outer", "inner", None, None, None),
        P(("outer", "inner"), None),
        P("outer", "inner", None),
    )
    out_specs = P(("outer", "inner"), None)
    return jax.shard_map(
        on_device, mesh=mesh, in_specs=in_specs, out_specs=out_specs, check_vma=False
    )
```

profile of v0, /device:TPU:1, one launch (start us, length us, event | category | flops | bytes accessed | tf_op | source)
XLA Modules:
  0.0 96.9 jit_solution(10595868039422779709)
XLA Ops:
  0.0 0.0 copy-start
  0.0 1.2 %copy-done = bf16[2048,256]{1,0:T(8,128)(2,1)S(1)} copy-done((bf16[2048,256]{1,0:T(8,128)(2,1)S(1)}, bf16[2048,256]{1,0:T(8,128)(2,1)}, u32[]{:S(2)}) %copy-start) | copy-done | bytes 1048600
  1.2 1.7 %convolution_convert_fusion.6 = bf16[8,256,256]{1,2,0:T(8,128)(2,1)S(1)} fusion(bf16[8,256,256]{2,1,0:T(8,128)(2,1)S(1)} %bitcast.63, bf16[8,256,256]{2,1,0:T(8,128)(2,1)} %bitcast.69), kind=kOutput, calls=%fused_computation.7 | convolution fusion | flops 268959744 | bytes 3145728 | tf_op jit(solution)/shard_map/klc,klr->kcr/dot_general | solution.py:39
  3.0 3.3 %collective-permute-start = (bf16[4,256,256]{1,2,0:T(8,128)(2,1)S(1)}, bf16[4,256,256]{1,2,0:T(8,128)(2,1)S(1)}, u32[]{:S(2)}, u32[]{:S(2)}) collective-permute-start(bf16[4,256,256]{1,2,0:T(8,128)(2,1)S(1)} %constant_dynamic-slice_fusion.6), channel_id=1, source_target_pairs={{0,1},{1,0},{2,3},{3,2},{4,5},{5,4},{6,7},{7,6},{8,9},{9,8},{10,11... | collective-permute-start | bytes 1572872 | tf_op jit(solution)/shard_map/ppermute | solution.py:10
  6.3 5.7 %fusion.23 = (bf16[1,1,1,8,512,256]{5,4,3,2,1,0:T(8,128)(2,1)S(1)}, bf16[1,1,1,8,512,256]{5,4,3,2,1,0:T(8,128)(2,1)}, bf16[1,1,1,8,512,256]{5,4,3,2,1,0:T(8,128)(2,1)}, bf16[1,1,1,8,512,256]{5,4,3,2,1,0:T(8,128)(2,1)}) fusion(bf16[4,1,1,8,512,256]{5,4,3,2,1,0:T(8,128)(2,1)} %param.8), kind=kLoop, calls=%fused_computation.49 | loop fusion | bytes 16777216 | tf_op jit(solution)/shard_map/slice | solution.py:54
  11.9 0.0 collective-permute-done
  12.0 0.1 broadcast_select_fusion.1
  12.0 0.9 convolution_convert_fusion.5
  12.9 0.1 constant_dynamic-slice_fusion.5
  13.0 0.2 copy.26
  13.2 0.1 collective-permute-start.1
  13.4 0.2 copy.25
  13.6 0.0 copy-start.3
  13.6 13.2 %collective-permute-done.1 = bf16[4,256,256]{2,1,0:T(8,128)(2,1)S(1)} collective-permute-done((bf16[4,256,256]{2,1,0:T(8,128)(2,1)S(1)}, bf16[4,256,256]{2,1,0:T(8,128)(2,1)S(1)}, u32[]{:S(2)}, u32[]{:S(2)}) %collective-permute-start.1) | collective-permute-done | bytes 524320 | tf_op jit(solution)/shard_map/ppermute | solution.py:10
  26.8 0.1 broadcast_select_fusion.3
  26.9 0.0 copy-done.3
  26.9 0.9 convolution_convert_fusion.4
  27.8 0.1 constant_dynamic-slice_fusion.3
  27.9 0.2 copy.28
  28.1 0.1 collective-permute-start.2
  28.2 0.2 copy.27
  28.4 0.0 copy-start.2
  28.4 12.3 %collective-permute-done.2 = bf16[4,256,256]{2,1,0:T(8,128)(2,1)S(1)} collective-permute-done((bf16[4,256,256]{2,1,0:T(8,128)(2,1)S(1)}, bf16[4,256,256]{2,1,0:T(8,128)(2,1)S(1)}, u32[]{:S(2)}, u32[]{:S(2)}) %collective-permute-start.2) | collective-permute-done | bytes 524320 | tf_op jit(solution)/shard_map/ppermute | solution.py:10
  40.8 0.1 broadcast_select_fusion.5
  40.8 0.0 copy-done.2
  40.9 0.9 convolution_convert_fusion.3
  41.8 0.0 copy-start.4
  41.8 0.1 constant_dynamic-slice_fusion.1
  41.9 0.2 copy.30
  42.1 1.8 %collective-permute-start.3 = (bf16[4,256,256]{2,1,0:T(8,128)(2,1)S(1)}, bf16[4,256,256]{2,1,0:T(8,128)(2,1)S(1)}, u32[]{:S(2)}, u32[]{:S(2)}) collective-permute-start(bf16[4,256,256]{2,1,0:T(8,128)(2,1)S(1)} %copy.30), channel_id=1, source_target_pairs={{0,64},{32,96},{64,0},{96,32},{128,192},{160,224},{192,128},{224,1... | collective-permute-start | bytes 1572872 | tf_op jit(solution)/shard_map/ppermute | solution.py:10
  43.9 0.0 copy-done.4
  44.0 0.2 copy.29
  44.2 0.0 copy-start.1
  44.2 11.3 %collective-permute-done.3 = bf16[4,256,256]{2,1,0:T(8,128)(2,1)S(1)} collective-permute-done((bf16[4,256,256]{2,1,0:T(8,128)(2,1)S(1)}, bf16[4,256,256]{2,1,0:T(8,128)(2,1)S(1)}, u32[]{:S(2)}, u32[]{:S(2)}) %collective-permute-start.3) | collective-permute-done | bytes 524320 | tf_op jit(solution)/shard_map/ppermute | solution.py:10
  55.4 0.1 broadcast_select_fusion.7
  55.5 0.0 copy-done.1
  55.5 0.7 convolution_convert_fusion.2
  56.2 0.6 gather_fusion
  56.9 2.3 %convolution_convert_fusion = bf16[8,256,256]{1,2,0:T(8,128)(2,1)S(1)} fusion(bf16[8,256,256]{2,1,0:T(8,128)(2,1)} %bitcast.75, bf16[1,1,8,256,256]{4,3,2,1,0:T(8,128)(2,1)} %param.9, bf16[8,256,256]{2,1,0:T(8,128)(2,1)S(1)} %gather_fusion, pred[8]{0:T(512)(128)(4,1)S(1)} %compare_and_fusion), kind=kOutput, calls=%fused_computation.1 | convolution fusion | flops 538443776 | bytes 4194312 | tf_op jit(solution)/shard_map/klr,kcr->klc/dot_general | solution.py:63
  59.2 36.8 %all_to_all.5 = bf16[32,64,256]{2,1,0:T(8,128)(2,1)S(1)} all-to-all(bf16[32,64,256]{2,1,0:T(8,128)(2,1)S(1)} %bitcast.71), channel_id=1, replica_groups=mesh['outer'=8,'inner'=32] {'inner'}, dimensions={0} | all-to-all | bytes 2097152 | tf_op jit(solution)/shard_map/all_to_all | solution.py:67
  95.9 1.0 %copy.32 = bf16[2048,256]{1,0:T(8,128)(2,1)} copy(bf16[2048,256]{1,0:T(8,128)(2,1)S(1)} %bitcast.64) | data formatting | bytes 2097152
  (4 shorter events, 0.1 us)
Async XLA Ops:
  0.0 1.2 %copy-start = (bf16[2048,256]{1,0:T(8,128)(2,1)S(1)}, bf16[2048,256]{1,0:T(8,128)(2,1)}, u32[]{:S(2)}) copy-start(bf16[2048,256]{1,0:T(8,128)(2,1)} %param.6) | copy-start | bytes 3145732
  3.0 9.0 %collective-permute-start = (bf16[4,256,256]{1,2,0:T(8,128)(2,1)S(1)}, bf16[4,256,256]{1,2,0:T(8,128)(2,1)S(1)}, u32[]{:S(2)}, u32[]{:S(2)}) collective-permute-start(bf16[4,256,256]{1,2,0:T(8,128)(2,1)S(1)} %constant_dynamic-slice_fusion.6), channel_id=1, source_target_pairs={{0,1},{1,0},{2,3},{3,2},{4,5},{5,4},{6,7},{7,6},{8,9},{9,8},{10,11... | collective-permute-start | bytes 1572872 | tf_op jit(solution)/shard_map/ppermute | solution.py:10
  13.2 13.5 %collective-permute-start.1 = (bf16[4,256,256]{2,1,0:T(8,128)(2,1)S(1)}, bf16[4,256,256]{2,1,0:T(8,128)(2,1)S(1)}, u32[]{:S(2)}, u32[]{:S(2)}) collective-permute-start(bf16[4,256,256]{2,1,0:T(8,128)(2,1)S(1)} %copy.26), channel_id=1, source_target_pairs={{0,2},{1,3},{2,0},{3,1},{4,6},{5,7},{6,4},{7,5},{8,10},{9,11},{10,... | collective-permute-start | bytes 1572872 | tf_op jit(solution)/shard_map/ppermute | solution.py:10
  13.6 13.3 %copy-start.3 = (bf16[1,1,1,8,512,256]{5,4,3,2,1,0:T(8,128)(2,1)S(1)}, bf16[1,1,1,8,512,256]{5,4,3,2,1,0:T(8,128)(2,1)}, u32[]{:S(2)}) copy-start(bf16[1,1,1,8,512,256]{5,4,3,2,1,0:T(8,128)(2,1)} %get-tuple-element.6) | copy-start | bytes 6291460
  28.1 12.7 %collective-permute-start.2 = (bf16[4,256,256]{2,1,0:T(8,128)(2,1)S(1)}, bf16[4,256,256]{2,1,0:T(8,128)(2,1)S(1)}, u32[]{:S(2)}, u32[]{:S(2)}) collective-permute-start(bf16[4,256,256]{2,1,0:T(8,128)(2,1)S(1)} %copy.28), channel_id=1, source_target_pairs={{0,32},{32,0},{64,96},{96,64},{128,160},{160,128},{192,224},{224,1... | collective-permute-start | bytes 1572872 | tf_op jit(solution)/shard_map/ppermute | solution.py:10
  28.4 12.4 %copy-start.2 = (bf16[1,1,1,8,512,256]{5,4,3,2,1,0:T(8,128)(2,1)S(1)}, bf16[1,1,1,8,512,256]{5,4,3,2,1,0:T(8,128)(2,1)}, u32[]{:S(2)}) copy-start(bf16[1,1,1,8,512,256]{5,4,3,2,1,0:T(8,128)(2,1)} %get-tuple-element.8) | copy-start | bytes 6291460
  41.8 2.1 %copy-start.4 = (s32[1,1,8]{2,1,0:T(1,128)S(1)}, s32[1,1,8]{2,1,0:T(1,128)}, u32[]{:S(2)}) copy-start(s32[1,1,8]{2,1,0:T(1,128)} %param.11) | copy-start | bytes 100
  42.1 13.3 %collective-permute-start.3 = (bf16[4,256,256]{2,1,0:T(8,128)(2,1)S(1)}, bf16[4,256,256]{2,1,0:T(8,128)(2,1)S(1)}, u32[]{:S(2)}, u32[]{:S(2)}) collective-permute-start(bf16[4,256,256]{2,1,0:T(8,128)(2,1)S(1)} %copy.30), channel_id=1, source_target_pairs={{0,64},{32,96},{64,0},{96,32},{128,192},{160,224},{192,128},{224,1... | collective-permute-start | bytes 1572872 | tf_op jit(solution)/shard_map/ppermute | solution.py:10
  44.2 11.3 %copy-start.1 = (bf16[1,1,1,8,512,256]{5,4,3,2,1,0:T(8,128)(2,1)S(1)}, bf16[1,1,1,8,512,256]{5,4,3,2,1,0:T(8,128)(2,1)}, u32[]{:S(2)}) copy-start(bf16[1,1,1,8,512,256]{5,4,3,2,1,0:T(8,128)(2,1)} %get-tuple-element.7) | copy-start | bytes 6291460
where the time goes:
time: 98.2 us; the launch traced here: 96.9 us
  waiting for transfers between devices  36.8 us (37%)
  blocking collectives  36.8 us (37%)
  local copies, waits for them, and re-layouts  9.99 us (10%)
  matrix products  7.52 us (8%)
  starting transfers between devices  5.29 us (5%)
    ppermute x4, waiting for transfers between devices, swapped(): lax.ppermute(array, axis, [(i, i ^ 1 << apart) for i in range(lax.axis_si...  36.8 us
    all_to_all x1, blocking collectives, on_device(): lax.all_to_all(pieces, 'inner', split_axis=0, concat_axis=0, tiled=True)  36.8 us
    slice x1, local copies, waits for them, and re-layouts, on_device(): box_state = merge_level(kept_half, received, half_flag, weights[level_idx])  5.66 us
    ppermute x4, starting transfers between devices, swapped(): lax.ppermute(array, axis, [(i, i ^ 1 << apart) for i in range(lax.axis_si...  5.29 us
    dot_general x4, matrix products, merge_level(): jnp.einsum('kcs,kosr->kocr', stacked, paired_w, preferred_element_type=jn...  3.48 us
    unnamed x17, local copies, waits for them, and re-layouts  3.44 us
    dot_general x1, matrix products, on_device(): jnp.einsum('klr,kcr->klc', local_u, core_out, preferred_element_type=jnp....  2.32 us
  transfers between devices with their start and end apart: 4, of which 3 were waited for; matrix products, arithmetic and copies ran while one was open for 6% of the time, Pallas kernels for 0%

commit v1 on v0

v1 whole, which is shorter than its diff:
```python
import functools

import jax
import jax.numpy as jnp
from jax import lax
from jax.experimental import pallas as pl
from jax.experimental.pallas import tpu as pltpu
from jax.sharding import PartitionSpec as P

MESH = pl.DeviceIdType.MESH
F32 = jnp.float32
BF16 = jnp.bfloat16
LEVELS = 4
BOXES = 8
HALF = 4
RANK = 256
LEAF = 256
COLS = 256
CHUNKS = 4
WIDTH = COLS // CHUNKS
PEERS = 32
PIECE = BOXES * LEAF // PEERS

ORDER = (
    (0, 0), (0, 1), (0, 2), (0, 3),
    (1, 0), (1, 1), (2, 0), (1, 2), (2, 1), (1, 3),
    (3, 0), (2, 2), (3, 1), (2, 3), (3, 2), (3, 3),
)


def kernel(
    x_hbm, v_hbm, t_hbm, c_hbm, u_hbm, order_ref, out_ref,
    xv, vv, tv, cv, uv, s0, s1, s2, s3, s4, r0, r1, r2, r3, bx, rb,
    in_sem, lev_send, lev_recv, far_send, far_recv,
):
    outer = lax.axis_index("outer")
    inner = lax.axis_index("inner")
    states = (s0, s1, s2, s3, s4)
    arrivals = (r0, r1, r2, r3)

    def bit(value, place):
        return lax.rem(lax.div(value, 1 << place), 2)

    flags = (bit(inner, 0), bit(inner, 1), bit(outer, 0), bit(outer, 1))
    partners = (
        (outer, inner + (1 - 2 * flags[0])),
        (outer, inner + 2 * (1 - 2 * flags[1])),
        (outer + (1 - 2 * flags[2]), inner),
        (outer + 2 * (1 - 2 * flags[3]), inner),
    )

    my_box = lax.div(inner, HALF)
    my_quarter = lax.rem(inner, HALF)
    my_x = lax.div(my_box, 4)
    my_pair = lax.rem(my_box, 4)
    boxes_order = []
    for pair_step in (2, 1, 3, 0):
        for x_step in (1, 0):
            box = lax.rem(my_x + x_step, 2) * 4 + lax.rem(my_pair + pair_step, 4)
            quarters = []
            for step in (1, 2, 3, 0):
                quarter = lax.rem(my_quarter + step, 4)
                is_self = pair_step == 0 and x_step == 0 and step == 0
                quarters.append((quarter, is_self))
            boxes_order.append((box, quarters))

    loads = [
        pltpu.make_async_copy(src, dst, in_sem.at[n])
        for n, (src, dst) in enumerate(
            (
                (x_hbm, xv), (v_hbm, vv),
                (t_hbm.at[0], tv.at[0]), (t_hbm.at[1], tv.at[1]),
                (t_hbm.at[2], tv.at[2]), (t_hbm.at[3], tv.at[3]),
                (c_hbm, cv), (u_hbm, uv),
            )
        )
    ]
    for load in loads:
        load.start()

    barrier = pltpu.get_barrier_semaphore()
    greeted = 0
    for box, quarters in boxes_order:
        for quarter, is_self in quarters:
            if not is_self:
                pl.semaphore_signal(
                    barrier, inc=1, device_id=(outer, box * 4 + quarter), device_id_type=MESH
                )
                greeted += 1
    for partner in partners[2:]:
        pl.semaphore_signal(barrier, inc=1, device_id=partner, device_id_type=MESH)
        greeted += 1

    def level_copy(level, chunk):
        return pltpu.make_async_remote_copy(
            src_ref=states[level].at[chunk, pl.ds((1 - flags[level]) * HALF, HALF)],
            dst_ref=arrivals[level].at[chunk],
            send_sem=lev_send.at[level, chunk],
            recv_sem=lev_recv.at[level, chunk],
            device_id=partners[level],
            device_id_type=MESH,
        )

    def leaf(box):
        rows = pl.ds(pl.multiple_of(box * LEAF, LEAF), LEAF)
        made = lax.dot_general(
            xv[rows, :], vv[rows, :], (((0,), (0,)), ((), ())), preferred_element_type=F32
        ).astype(BF16)
        for chunk in range(CHUNKS):
            s0[chunk, box] = made[chunk * WIDTH : (chunk + 1) * WIDTH]

    loads[0].wait()
    loads[1].wait()
    for n in range(HALF):
        leaf((1 - flags[0]) * HALF + n)
    pl.semaphore_wait(barrier, greeted)
    for chunk in range(CHUNKS):
        level_copy(0, chunk).start()
    for n in range(HALF):
        leaf(flags[0] * HALF + n)

    def merge(level, chunk, pair):
        flag = flags[level]
        kept = states[level][chunk, flag * HALF + pair]
        came = arrivals[level][chunk, pair]
        for o in range(2):
            box = 2 * pair + o
            kept_w = tv[level, box, pl.ds(pl.multiple_of(flag * RANK, RANK), RANK), :]
            came_w = tv[level, box, pl.ds(pl.multiple_of((1 - flag) * RANK, RANK), RANK), :]
            total = jnp.dot(kept, kept_w, preferred_element_type=F32)
            total = total + jnp.dot(came, came_w, preferred_element_type=F32)
            states[level + 1][chunk, box] = total.astype(BF16)

    def far_copy(chunk, box, quarter):
        peer = box * 4 + quarter
        return pltpu.make_async_remote_copy(
            src_ref=bx.at[chunk, peer],
            dst_ref=rb.at[chunk, inner],
            send_sem=far_send.at[chunk, peer],
            recv_sem=far_recv.at[chunk, inner],
            device_id=(outer, peer),
            device_id_type=MESH,
        )

    def far_arrival(chunk, peer):
        return pltpu.make_async_remote_copy(
            src_ref=bx.at[chunk, peer],
            dst_ref=rb.at[chunk, peer],
            send_sem=far_send.at[chunk, peer],
            recv_sem=far_recv.at[chunk, peer],
            device_id=(outer, peer),
            device_id_type=MESH,
        )

    def finish(chunk):
        for box, quarters in boxes_order:
            chosen = s4[chunk, order_ref[box]]
            core = jnp.dot(chosen, cv[box], preferred_element_type=F32).astype(BF16)
            rows = pl.ds(pl.multiple_of(box * LEAF, LEAF), LEAF)
            made = lax.dot_general(
                uv[rows, :], core, (((1,), (1,)), ((), ())), preferred_element_type=F32
            )
            for quarter in range(4):
                at = quarter * PIECE
                packed = jnp.concatenate(
                    [made[at : at + PIECE // 2], made[at + PIECE // 2 : at + PIECE]], axis=1
                ).astype(BF16)
                bx[chunk, box * 4 + quarter] = packed
            for quarter, is_self in quarters:
                if is_self:
                    rb[chunk, inner] = bx[chunk, inner]
                else:
                    far_copy(chunk, box, quarter).start()

    waited = set()
    for level, chunk in ORDER:
        if level not in waited:
            waited.add(level)
            loads[2 + level].wait()
        copy = level_copy(level, chunk)
        copy.wait()
        if level < LEVELS - 1:
            later = flags[level + 1]
            for n in range(2):
                merge(level, chunk, (1 - later) * 2 + n)
            level_copy(level + 1, chunk).start()
            for n in range(2):
                merge(level, chunk, later * 2 + n)
        else:
            for n in range(HALF):
                merge(level, chunk, n)
            if chunk == 0:
                loads[6].wait()
                loads[7].wait()
            finish(chunk)

    lane = lax.broadcasted_iota(jnp.int32, (PIECE // 2, 128), 1)
    for duo in range(CHUNKS // 2):
        for chunk in (2 * duo, 2 * duo + 1):
            for box, quarters in boxes_order:
                for quarter, is_self in quarters:
                    if not is_self:
                        far_arrival(chunk, box * 4 + quarter).wait()

        def unpack(peer, carry):
            first = rb[2 * duo, peer].astype(F32)
            second = rb[2 * duo + 1, peer].astype(F32)
            low = jnp.where(lane < WIDTH, first, pltpu.roll(second, WIDTH, 1))
            high = jnp.where(lane < WIDTH, pltpu.roll(first, WIDTH, 1), second)
            base = pl.multiple_of(peer * PIECE, PIECE)
            cols = slice(duo * 128, duo * 128 + 128)
            out_ref[pl.ds(base, PIECE // 2), cols] = low.astype(BF16)
            out_ref[pl.ds(base + PIECE // 2, PIECE // 2), cols] = high.astype(BF16)
            return carry

        lax.fori_loop(0, PEERS, unpack, 0)


def on_device(vectors, leaf_basis, transfer, core_mats, row_basis, box_order):
    any_space = pl.BlockSpec(memory_space=pl.ANY)
    call = pl.pallas_call(
        kernel,
        out_shape=jax.ShapeDtypeStruct((BOXES * LEAF, COLS), BF16),
        in_specs=[any_space] * 5 + [pl.BlockSpec(memory_space=pltpu.SMEM)],
        out_specs=pl.BlockSpec(memory_space=pltpu.VMEM),
        scratch_shapes=[
            pltpu.VMEM((BOXES * LEAF, COLS), BF16),
            pltpu.VMEM((BOXES * LEAF, RANK), BF16),
            pltpu.VMEM((LEVELS, BOXES, 2 * RANK, RANK), BF16),
            pltpu.VMEM((BOXES, RANK, RANK), BF16),
            pltpu.VMEM((BOXES * LEAF, RANK), BF16),
        ]
        + [pltpu.VMEM((CHUNKS, BOXES, WIDTH, RANK), BF16)] * 5
        + [pltpu.VMEM((CHUNKS, HALF, WIDTH, RANK), BF16)] * 4
        + [
            pltpu.VMEM((CHUNKS, PEERS, PIECE // 2, 128), BF16),
            pltpu.VMEM((CHUNKS, PEERS, PIECE // 2, 128), BF16),
            pltpu.SemaphoreType.DMA((8,)),
            pltpu.SemaphoreType.DMA((LEVELS, CHUNKS)),
            pltpu.SemaphoreType.DMA((LEVELS, CHUNKS)),
            pltpu.SemaphoreType.DMA((CHUNKS, PEERS)),
            pltpu.SemaphoreType.DMA((CHUNKS, PEERS)),
        ],
        compiler_params=pltpu.CompilerParams(
            collective_id=0, has_side_effects=True, vmem_limit_bytes=60 * 1024 * 1024
        ),
        name="butterfly",
    )
    return call(
        vectors,
        leaf_basis,
        transfer.reshape(LEVELS, BOXES, 2 * RANK, RANK),
        core_mats.reshape(BOXES, RANK, RANK),
        row_basis,
        box_order.reshape(BOXES),
    )


def solution(mesh):
    in_specs = (
        P(("outer", "inner"), None),
        P(("outer", "inner"), None),
        P(None, "outer", "inner", None, None, None),
        P("outer", "inner", None, None, None),
        P(("outer", "inner"), None),
        P("outer", "inner", None),
    )
    out_specs = P(("outer", "inner"), None)
    return jax.shard_map(
        on_device, mesh=mesh, in_specs=in_specs, out_specs=out_specs, check_vma=False
    )
```

time: 98.2 us -> 62.4 us (0.64); the launches traced: 96.9 us -> 62.3 us
  Pallas kernels: 0 us -> 60 us
  blocking collectives: 36.8 us -> 0 us
  waiting for transfers between devices: 36.8 us -> 0 us
  local copies, waits for them, and re-layouts: 9.99 us -> 2.26 us
  matrix products: 7.52 us -> 0 us
  starting transfers between devices: 5.29 us -> 0 us
    pallas_call x0 -> x1, Pallas kernels: none -> 60 us  [on_device(): call(vectors, leaf_basis, transfer.reshape(LEVELS, BOXES, 2 * RANK, RANK)...]
    ppermute x4 -> x0, waiting for transfers between devices: 36.8 us -> none  [swapped(): lax.ppermute(array, axis, [(i, i ^ 1 << apart) for i in range(lax.axis_si...]
    all_to_all x1 -> x0, blocking collectives: 36.8 us -> none  [on_device(): lax.all_to_all(pieces, 'inner', split_axis=0, concat_axis=0, tiled=True)]
    dot_general x6 -> x0, matrix products: 7.52 us -> none  [the longest x4 3.48 us: merge_level(): jnp.einsum('kcs,kosr->kocr', stacked, paired_w, preferred_element_type=jn...]
    slice x1 -> x0, local copies, waits for them, and re-layouts: 5.66 us -> none  [on_device(): box_state = merge_level(kept_half, received, half_flag, weights[level_idx])]
    ppermute x4 -> x0, starting transfers between devices: 5.29 us -> none  [swapped(): lax.ppermute(array, axis, [(i, i ^ 1 << apart) for i in range(lax.axis_si...]
    unnamed x17 -> x1, local copies, waits for them, and re-layouts: 3.44 us -> 2.26 us
  transfers between devices with their start and end apart: 4 -> 0, of which waited for: 3 -> 0; matrix products, arithmetic and copies ran while one was open for 6% -> 0% of each run, Pallas kernels for 0% -> 0%
where the time goes in v1:
time: 62.4 us; the launch traced here: 62.3 us
  Pallas kernels  60 us (96%)
  local copies, waits for them, and re-layouts  2.26 us (4%)
    pallas_call x1, Pallas kernels, on_device(): call(vectors, leaf_basis, transfer.reshape(LEVELS, BOXES, 2 * RANK, RANK)...  60 us
    unnamed x1, local copies, waits for them, and re-layouts  2.26 us

profile of v1, /device:TPU:1, one launch (start us, length us, event | category | flops | bytes accessed | tf_op | source)
XLA Modules:
  0.0 62.3 jit_solution(4267359688256189770)
XLA Ops:
  0.0 60.0 %butterfly.1 = bf16[2048,256]{1,0:T(8,128)(2,1)} custom-call(bf16[2048,256]{1,0:T(8,128)(2,1)} %x_hbm.1, bf16[2048,256]{1,0:T(8,128)(2,1)} %v_hbm.1, bf16[4,8,512,256]{3,2,1,0:T(8,128)(2,1)} %bitcast.3, bf16[8,256,256]{2,1,0:T(8,128)(2,1)} %bitcast.4, bf16[2048,256]{1,0:T(8,128)(2,1)} %u_hbm.1, s32[8]{0:T(128)} %bitcast.5), custom_call_target="tpu_custom_call" | custom-call | tf_op jit(solution)/shard_map/butterfly/pallas_call | solution.py:249
  60.0 2.3 %copy.8 = bf16[2048,256]{1,0:T(8,128)(2,1)} copy(bf16[2048,256]{1,0:T(8,128)(2,1)} %butterfly.1) | data formatting | bytes 2097152

commit v2 on v1

v2 whole, which is shorter than its diff:
```python
import functools

import jax
import jax.numpy as jnp
from jax import lax
from jax.experimental import pallas as pl
from jax.experimental.pallas import tpu as pltpu
from jax.sharding import PartitionSpec as P

MESH = pl.DeviceIdType.MESH
F32 = jnp.float32
BF16 = jnp.bfloat16
LEVELS = 4
BOXES = 8
HALF = 4
RANK = 256
LEAF = 256
COLS = 256
CHUNKS = ((0, 32), (64, 64), (128, 64), (192, 64), (32, 32))
COUNT = len(CHUNKS)
LANES = 128
KERNEL_VMEM = 65_600_000
PEERS = 32
PIECE = BOXES * LEAF // PEERS
PIECE_ROWS = tuple(PIECE * width // LANES for _, width in CHUNKS)
PIECE_AT = tuple(sum(PIECE_ROWS[:c]) for c in range(COUNT))
ALL_ROWS = sum(PIECE_ROWS)

STEPS = (
    ("m", 0, 0, 0), ("s", 1, 0), ("m", 0, 0, 1), ("m", 0, 1, 0), ("s", 1, 1), ("m", 0, 1, 1),
    ("m", 0, 2, 0), ("s", 1, 2), ("m", 0, 2, 1), ("m", 0, 3, 0), ("s", 1, 3), ("m", 0, 3, 1),
    ("m", 0, 4, 0), ("s", 1, 4), ("m", 0, 4, 1), ("m", 1, 0, 0), ("s", 2, 0), ("m", 1, 0, 1),
    ("m", 2, 0, 0), ("s", 3, 0), ("m", 1, 1, 0), ("s", 2, 1), ("m", 1, 1, 1), ("m", 2, 0, 1),
    ("m", 1, 2, 0), ("m", 1, 2, 1), ("m", 2, 1, 0), ("s", 3, 1), ("s", 2, 2), ("m", 3, 0, 0),
    ("m", 3, 0, 1), ("f", 0), ("m", 2, 1, 1), ("m", 1, 3, 0), ("m", 1, 3, 1), ("m", 1, 4, 0),
    ("m", 1, 4, 1), ("m", 2, 2, 0), ("s", 3, 2), ("s", 2, 3), ("m", 3, 1, 0), ("m", 3, 1, 1),
    ("f", 1), ("m", 2, 2, 1), ("m", 2, 3, 0), ("s", 3, 3), ("s", 2, 4), ("m", 3, 2, 0),
    ("m", 3, 2, 1), ("f", 2), ("m", 2, 3, 1), ("m", 2, 4, 0), ("s", 3, 4), ("m", 3, 3, 0),
    ("m", 3, 3, 1), ("f", 3), ("m", 2, 4, 1), ("m", 3, 4, 0), ("m", 3, 4, 1), ("f", 4),
)


def kernel(
    x_hbm, v_hbm, t_hbm, c_hbm, u_hbm, order_ref, rb,
    xv, vv, tv, cv, uv, bx, *rest,
):
    outer = lax.axis_index("outer")
    inner = lax.axis_index("inner")
    rest = list(rest)

    def take(count):
        taken, rest[:] = rest[:count], rest[count:]
        return taken

    states = [take(COUNT) for _ in range(LEVELS + 1)]
    arrivals = [take(COUNT) for _ in range(LEVELS)]
    cores = take(COUNT)
    in_sem, own_sem, lev_send, lev_recv, far_send, far_recv = rest

    def bit(value, place):
        return lax.rem(lax.div(value, 1 << place), 2)

    flags = (bit(inner, 0), bit(inner, 1), bit(outer, 0), bit(outer, 1))
    partners = (
        (outer, inner + (1 - 2 * flags[0])),
        (outer, inner + 2 * (1 - 2 * flags[1])),
        (outer + (1 - 2 * flags[2]), inner),
        (outer + 2 * (1 - 2 * flags[3]), inner),
    )

    my_box = lax.div(inner, HALF)
    my_quarter = lax.rem(inner, HALF)
    my_x = lax.div(my_box, 4)
    my_pair = lax.rem(my_box, 4)
    boxes_order = []
    for pair_step in (2, 1, 3, 0):
        for x_step in (1, 0):
            box = lax.rem(my_x + x_step, 2) * 4 + lax.rem(my_pair + pair_step, 4)
            quarters = []
            for step in (1, 2, 3, 0):
                quarter = lax.rem(my_quarter + step, 4)
                is_self = pair_step == 0 and x_step == 0 and step == 0
                quarters.append((quarter, is_self))
            boxes_order.append((box, quarters))

    def half_rows(side):
        return pl.ds(pl.multiple_of(side * (HALF * LEAF), HALF * LEAF), HALF * LEAF)

    sent_rows, kept_rows = half_rows(1 - flags[0]), half_rows(flags[0])
    loads = [
        pltpu.make_async_copy(src, dst, in_sem.at[n])
        for n, (src, dst) in enumerate(
            (
                (t_hbm.at[0], tv.at[0]), (t_hbm.at[1], tv.at[1]),
                (t_hbm.at[2], tv.at[2]), (t_hbm.at[3], tv.at[3]),
                (c_hbm, cv), (u_hbm, uv),
                (x_hbm.at[sent_rows], xv.at[sent_rows]), (v_hbm.at[sent_rows], vv.at[sent_rows]),
                (x_hbm.at[kept_rows], xv.at[kept_rows]), (v_hbm.at[kept_rows], vv.at[kept_rows]),
            )
        )
    ]
    for n in (6, 7):
        loads[n].start()

    barrier = pltpu.get_barrier_semaphore()
    greeted = 0
    for box, quarters in boxes_order:
        for quarter, is_self in quarters:
            if not is_self:
                pl.semaphore_signal(
                    barrier, inc=1, device_id=(outer, box * 4 + quarter), device_id_type=MESH
                )
                greeted += 1
    for partner in partners[2:]:
        pl.semaphore_signal(barrier, inc=1, device_id=partner, device_id_type=MESH)
        greeted += 1

    def first_pair(level, half):
        if level < LEVELS - 1:
            later = flags[level + 1]
            return 2 * (1 - later) if half == 0 else 2 * later
        return 2 * half

    def level_copy(level, chunk, half):
        halves = level in (1, 2)
        at, size = (first_pair(level, half), 2) if halves else (0, HALF)
        return pltpu.make_async_remote_copy(
            src_ref=states[level][chunk].at[pl.ds((1 - flags[level]) * HALF + at, size)],
            dst_ref=arrivals[level][chunk].at[pl.ds(at, size)],
            send_sem=lev_send.at[level, chunk],
            recv_sem=lev_recv.at[level, chunk, half],
            device_id=partners[level],
            device_id_type=MESH,
        )

    def send(level, chunk):
        level_copy(level, chunk, 0).start()
        if level in (1, 2):
            level_copy(level, chunk, 1).start()

    def leaf(box):
        rows = pl.ds(pl.multiple_of(box * LEAF, LEAF), LEAF)
        made = lax.dot_general(
            xv[rows, :], vv[rows, :], (((0,), (0,)), ((), ())), preferred_element_type=F32
        ).astype(BF16)
        for chunk, (at, width) in enumerate(CHUNKS):
            states[0][chunk][box] = made[at : at + width]

    with jax.named_scope("load"):
        loads[6].wait()
        loads[7].wait()
    for n in (8, 9, 0):
        loads[n].start()
    for n in range(HALF):
        leaf((1 - flags[0]) * HALF + n)
    with jax.named_scope("greet"):
        pl.semaphore_wait(barrier, greeted)
    for chunk in range(COUNT):
        send(0, chunk)
    for n in (1, 2, 3, 4, 5):
        loads[n].start()
    loads[8].wait()
    loads[9].wait()
    for n in range(HALF):
        leaf(flags[0] * HALF + n)

    def merge(level, chunk, pair):
        flag = flags[level]
        kept = states[level][chunk][flag * HALF + pair]
        came = arrivals[level][chunk][pair]
        for o in range(2):
            box = 2 * pair + o
            kept_w = tv[level, box, pl.ds(pl.multiple_of(flag * RANK, RANK), RANK), :]
            came_w = tv[level, box, pl.ds(pl.multiple_of((1 - flag) * RANK, RANK), RANK), :]
            total = jnp.dot(kept, kept_w, preferred_element_type=F32)
            total = total + jnp.dot(came, came_w, preferred_element_type=F32)
            states[level + 1][chunk][box] = total.astype(BF16)

    def far_copy(chunk, box, quarter):
        peer = box * 4 + quarter
        rows = pl.ds(PIECE_AT[chunk], PIECE_ROWS[chunk])
        return pltpu.make_async_remote_copy(
            src_ref=bx.at[peer, rows],
            dst_ref=rb.at[inner, rows],
            send_sem=far_send.at[0],
            recv_sem=far_recv.at[chunk],
            device_id=(outer, peer),
            device_id_type=MESH,
        )

    own = [
        pltpu.make_async_copy(
            bx.at[inner, pl.ds(at, rows)], rb.at[inner, pl.ds(at, rows)], own_sem.at[0]
        )
        for at, rows in zip(PIECE_AT, PIECE_ROWS)
    ]

    def finish(chunk):
        size = PIECE_ROWS[chunk]
        at = PIECE_AT[chunk]
        core = cores[chunk]
        for box, _ in boxes_order:
            core[box] = jnp.dot(
                states[LEVELS][chunk][order_ref[box]], cv[box], preferred_element_type=F32
            ).astype(BF16)
        for box, quarters in boxes_order:
            rows = pl.ds(pl.multiple_of(box * LEAF, LEAF), LEAF)
            made = jnp.dot(uv[rows, :], core[box].T, preferred_element_type=F32)
            for quarter in range(4):
                groups = [
                    made[first : first + size]
                    for first in range(quarter * PIECE, (quarter + 1) * PIECE, size)
                ]
                bx[box * 4 + quarter, at : at + size] = jnp.concatenate(groups, axis=1).astype(BF16)
        with jax.named_scope("go"):
            for box, quarters in boxes_order:
                for quarter, is_self in quarters:
                    if is_self:
                        own[chunk].start()
                    else:
                        far_copy(chunk, box, quarter).start()

    loaded = set()

    def need(n):
        if n not in loaded:
            loaded.add(n)
            loads[n].wait()

    for kind, *numbers in STEPS:
        if kind == "m":
            level, chunk, half = numbers
            need(level)
            if half == 0 or level in (1, 2):
                with jax.named_scope(f"w{level}{chunk}{half}"):
                    level_copy(level, chunk, half).wait_recv()
            for n in range(2):
                merge(level, chunk, first_pair(level, half) + n)
        elif kind == "s":
            send(*numbers)
        else:
            need(4)
            need(5)
            with jax.named_scope(f"f{numbers[0]}"):
                finish(*numbers)

    for chunk in range(COUNT):
        with jax.named_scope(f"far{chunk}"):
            arrived = rb.at[pl.ds(0, PEERS - 1), pl.ds(PIECE_AT[chunk], PIECE_ROWS[chunk])]
            pltpu.make_async_copy(arrived, arrived, far_recv.at[chunk]).wait()
    with jax.named_scope("drain"):
        pltpu.make_async_copy(rb.at[0], rb.at[0], own_sem.at[0]).wait()
        sent = bx.at[pl.ds(0, PEERS - 1)]
        pltpu.make_async_copy(sent, sent, far_send.at[0]).wait()
        for level in range(LEVELS):
            for chunk in range(COUNT):
                moved = arrivals[level][chunk]
                pltpu.make_async_copy(moved, moved, lev_send.at[level, chunk]).wait()


def unpack(rb, out, ready, out_sem):
    groups = 4
    peers = PEERS // groups
    rows = peers * PIECE
    outs = [
        pltpu.make_async_copy(
            ready.at[pl.ds(g * rows, rows)], out.at[pl.ds(g * rows, rows)], out_sem.at[g]
        )
        for g in range(groups)
    ]
    step = min(PIECE_ROWS)
    lane = lax.broadcasted_iota(jnp.int32, (step, LANES), 1)
    for g in range(groups):
        for peer in range(g * peers, (g + 1) * peers):
            for block in range(0, COLS, LANES):
                for row in range(0, PIECE, step):
                    total = None
                    for chunk, (at, width) in enumerate(CHUNKS):
                        if not block <= at < block + LANES:
                            continue
                        group, inside = divmod(row, PIECE_ROWS[chunk])
                        first = PIECE_AT[chunk] + inside
                        part = rb[peer, first : first + step].astype(F32)
                        turn = (at - block - group * width) % LANES
                        part = pltpu.roll(part, turn, 1) if turn else part
                        mine = (lane >= at - block) & (lane < at - block + width)
                        total = part if total is None else jnp.where(mine, part, total)
                    base = peer * PIECE + row
                    ready[base : base + step, block : block + LANES] = total.astype(BF16)
        outs[g].start()
    with jax.named_scope("outs"):
        for copy in outs:
            copy.wait()


def on_device(vectors, leaf_basis, transfer, core_mats, row_basis, box_order):
    any_space = pl.BlockSpec(memory_space=pl.ANY)
    vmem = pl.BlockSpec(memory_space=pltpu.VMEM)
    call = pl.pallas_call(
        kernel,
        out_shape=pltpu.VMEM((PEERS, ALL_ROWS, LANES), BF16),
        in_specs=[any_space] * 5 + [pl.BlockSpec(memory_space=pltpu.SMEM)],
        out_specs=vmem,
        scratch_shapes=[
            pltpu.VMEM((BOXES * LEAF, COLS), BF16),
            pltpu.VMEM((BOXES * LEAF, RANK), BF16),
            pltpu.VMEM((LEVELS, BOXES, 2 * RANK, RANK), BF16),
            pltpu.VMEM((BOXES, RANK, RANK), BF16),
            pltpu.VMEM((BOXES * LEAF, RANK), BF16),
            pltpu.VMEM((PEERS, ALL_ROWS, LANES), BF16),
        ]
        + [pltpu.VMEM((BOXES, width, RANK), BF16) for _, width in CHUNKS] * (LEVELS + 1)
        + [pltpu.VMEM((HALF, width, RANK), BF16) for _, width in CHUNKS] * LEVELS
        + [pltpu.VMEM((BOXES, width, RANK), BF16) for _, width in CHUNKS]
        + [
            pltpu.SemaphoreType.DMA((10,)),
            pltpu.SemaphoreType.DMA((1,)),
            pltpu.SemaphoreType.DMA((LEVELS, COUNT)),
            pltpu.SemaphoreType.DMA((LEVELS, COUNT, 2)),
            pltpu.SemaphoreType.DMA((1,)),
            pltpu.SemaphoreType.DMA((COUNT,)),
        ],
        compiler_params=pltpu.CompilerParams(
            collective_id=0, has_side_effects=True, vmem_limit_bytes=KERNEL_VMEM
        ),
        name="butterfly",
    )
    arrived = call(
        vectors,
        leaf_basis,
        transfer.reshape(LEVELS, BOXES, 2 * RANK, RANK),
        core_mats.reshape(BOXES, RANK, RANK),
        row_basis,
        box_order.reshape(BOXES),
    )
    return pl.pallas_call(
        unpack,
        out_shape=jax.ShapeDtypeStruct((BOXES * LEAF, COLS), BF16),
        in_specs=[vmem],
        out_specs=any_space,
        scratch_shapes=[pltpu.VMEM((BOXES * LEAF, COLS), BF16), pltpu.SemaphoreType.DMA((4,))],
        compiler_params=pltpu.CompilerParams(vmem_limit_bytes=8 * 1024 * 1024),
        name="unpack",
    )(arrived)


def solution(mesh):
    in_specs = (
        P(("outer", "inner"), None),
        P(("outer", "inner"), None),
        P(None, "outer", "inner", None, None, None),
        P("outer", "inner", None, None, None),
        P(("outer", "inner"), None),
        P("outer", "inner", None),
    )
    out_specs = P(("outer", "inner"), None)
    return jax.shard_map(
        on_device, mesh=mesh, in_specs=in_specs, out_specs=out_specs, check_vma=False
    )
```

time: 62.4 us -> 53.5 us (0.86)
  Pallas kernels: 60 us -> 53.4 us
  local copies, waits for them, and re-layouts: 2.26 us -> 0 us
    pallas_call x1, Pallas kernels: 60 us -> 52.2 us  [on_device(): call(vectors, leaf_basis, transfer.reshape(LEVELS, BOXES, 2 * RANK, RANK)...]
    unnamed x1 -> x0, local copies, waits for them, and re-layouts: 2.26 us -> none
    pallas_call x0 -> x1, Pallas kernels: none -> 1.24 us  [on_device(): pl.pallas_call(unpack, out_shape=jax.ShapeDtypeStruct((BOXES * LEAF, COLS...]
where the time goes in v2:
time: 53.5 us; the launch traced here: 53.4 us
  Pallas kernels  53.4 us (100%)
    pallas_call x1, Pallas kernels, on_device(): call(vectors, leaf_basis, transfer.reshape(LEVELS, BOXES, 2 * RANK, RANK)...  52.2 us
    pallas_call x1, Pallas kernels, on_device(): pl.pallas_call(unpack, out_shape=jax.ShapeDtypeStruct((BOXES * LEAF, COLS...  1.24 us

profile of v2, /device:TPU:1, one launch (start us, length us, event | category | flops | bytes accessed | tf_op | source)
XLA Modules:
  0.0 53.4 jit_solution(9444679448307652223)
XLA Ops:
  0.0 52.2 %butterfly.1.rb = bf16[32,128,128]{2,1,0:T(8,128)(2,1)S(1)} custom-call(bf16[2048,256]{1,0:T(8,128)(2,1)} %x_hbm.1, bf16[2048,256]{1,0:T(8,128)(2,1)} %v_hbm.1, bf16[4,8,512,256]{3,2,1,0:T(8,128)(2,1)} %bitcast.3, bf16[8,256,256]{2,1,0:T(8,128)(2,1)} %bitcast.4, bf16[2048,256]{1,0:T(8,128)(2,1)} %u_hbm.1, s32[8]{0:T(128)} %bitcast.5), custom_call_target="tpu_custom_call" | custom-call | tf_op jit(solution)/shard_map/butterfly/pallas_call | solution.py:328
  52.2 1.2 %unpack.1 = bf16[2048,256]{1,0:T(8,128)(2,1)} custom-call(bf16[32,128,128]{2,1,0:T(8,128)(2,1)S(1)} %butterfly.1.rb), custom_call_target="tpu_custom_call" | custom-call | tf_op jit(solution)/shard_map/unpack/pallas_call | solution.py:336

commit v3 on v2

--- a/solution.py
+++ b/solution.py
@@ -29,14 +29,16 @@
 STEPS = (
     ("m", 0, 0, 0), ("s", 1, 0), ("m", 0, 0, 1), ("m", 0, 1, 0), ("s", 1, 1), ("m", 0, 1, 1),
     ("m", 0, 2, 0), ("s", 1, 2), ("m", 0, 2, 1), ("m", 0, 3, 0), ("s", 1, 3), ("m", 0, 3, 1),
-    ("m", 0, 4, 0), ("s", 1, 4), ("m", 0, 4, 1), ("m", 1, 0, 0), ("s", 2, 0), ("m", 1, 0, 1),
-    ("m", 2, 0, 0), ("s", 3, 0), ("m", 1, 1, 0), ("s", 2, 1), ("m", 1, 1, 1), ("m", 2, 0, 1),
-    ("m", 1, 2, 0), ("m", 1, 2, 1), ("m", 2, 1, 0), ("s", 3, 1), ("s", 2, 2), ("m", 3, 0, 0),
-    ("m", 3, 0, 1), ("f", 0), ("m", 2, 1, 1), ("m", 1, 3, 0), ("m", 1, 3, 1), ("m", 1, 4, 0),
-    ("m", 1, 4, 1), ("m", 2, 2, 0), ("s", 3, 2), ("s", 2, 3), ("m", 3, 1, 0), ("m", 3, 1, 1),
-    ("f", 1), ("m", 2, 2, 1), ("m", 2, 3, 0), ("s", 3, 3), ("s", 2, 4), ("m", 3, 2, 0),
-    ("m", 3, 2, 1), ("f", 2), ("m", 2, 3, 1), ("m", 2, 4, 0), ("s", 3, 4), ("m", 3, 3, 0),
-    ("m", 3, 3, 1), ("f", 3), ("m", 2, 4, 1), ("m", 3, 4, 0), ("m", 3, 4, 1), ("f", 4),
+    ("m", 0, 4, 0), ("s", 1, 4), ("m", 0, 4, 1), ("r", 1), ("m", 1, 0, 0), ("s", 2, 0),
+    ("m", 1, 0, 1), ("r", 2), ("m", 1, 1, 0), ("h", 2, 1, 0), ("m", 2, 0, 0), ("s", 3, 0),
+    ("h", 2, 1, 1), ("m", 1, 1, 1), ("m", 2, 0, 1), ("m", 1, 2, 0), ("m", 2, 1, 0),
+    ("s", 3, 1), ("h", 2, 2, 0), ("h", 2, 2, 1), ("m", 1, 2, 1), ("m", 1, 3, 0), ("r", 3),
+    ("m", 3, 0, 0), ("m", 3, 0, 1), ("f", 0), ("m", 1, 3, 1), ("m", 1, 4, 0), ("m", 1, 4, 1),
+    ("m", 2, 1, 1), ("m", 2, 2, 0), ("s", 3, 2), ("h", 2, 3, 0), ("h", 2, 3, 1),
+    ("h", 2, 4, 0), ("h", 2, 4, 1), ("m", 3, 1, 0), ("m", 3, 1, 1), ("f", 1), ("m", 2, 2, 1),
+    ("m", 3, 2, 0), ("m", 3, 2, 1), ("f", 2), ("m", 2, 3, 0), ("s", 3, 3), ("m", 2, 3, 1),
+    ("m", 2, 4, 0), ("s", 3, 4), ("m", 2, 4, 1), ("m", 3, 3, 0), ("m", 3, 3, 1), ("f", 3),
+    ("m", 3, 4, 0), ("m", 3, 4, 1), ("f", 4),
 )
 
 
@@ -55,7 +57,7 @@
     states = [take(COUNT) for _ in range(LEVELS + 1)]
     arrivals = [take(COUNT) for _ in range(LEVELS)]
     cores = take(COUNT)
-    in_sem, own_sem, lev_send, lev_recv, far_send, far_recv = rest
+    in_sem, own_sem, lev_send, lev_recv, far_send, far_recv, ready = rest
 
     def bit(value, place):
         return lax.rem(lax.div(value, 1 << place), 2)
@@ -103,17 +105,24 @@
         loads[n].start()
 
     barrier = pltpu.get_barrier_semaphore()
-    greeted = 0
-    for box, quarters in boxes_order:
-        for quarter, is_self in quarters:
-            if not is_self:
-                pl.semaphore_signal(
-                    barrier, inc=1, device_id=(outer, box * 4 + quarter), device_id_type=MESH
-                )
-                greeted += 1
-    for partner in partners[2:]:
-        pl.semaphore_signal(barrier, inc=1, device_id=partner, device_id_type=MESH)
-        greeted += 1
+
+    def place(x_step, z_step, core_step):
+        x = lax.rem(lax.div(inner, 16) + x_step, 2)
+        z = lax.rem(lax.div(inner, 2) + z_step + 8, 8)
+        return outer, x * 16 + z * 2 + lax.rem(inner + core_step, 2)
+
+    near = [place(0, 0, 1), place(0, 1, 0), place(0, -1, 0), place(1, 0, 0)]
+    rounds = (
+        near,
+        [place(1, 0, 1), place(0, 2, 0), place(0, -2, 0)],
+        [place(0, 0, 1), place(1, 0, 0), place(1, 0, 1)],
+    )
+
+    def signal(semaphore, devices):
+        for device in devices:
+            pl.semaphore_signal(semaphore, inc=1, device_id=device, device_id_type=MESH)
+
+    signal(barrier, [*near, *partners[2:]])
 
     def first_pair(level, half):
         if level < LEVELS - 1:
@@ -127,8 +136,8 @@
         return pltpu.make_async_remote_copy(
             src_ref=states[level][chunk].at[pl.ds((1 - flags[level]) * HALF + at, size)],
             dst_ref=arrivals[level][chunk].at[pl.ds(at, size)],
-            send_sem=lev_send.at[level, chunk],
-            recv_sem=lev_recv.at[level, chunk, half],
+            send_sem=lev_send.at[0],
+            recv_sem=lev_recv.at[(0, 5, 15, 25)[level] + chunk + COUNT * half],
             device_id=partners[level],
             device_id_type=MESH,
         )
@@ -154,9 +163,10 @@
     for n in range(HALF):
         leaf((1 - flags[0]) * HALF + n)
     with jax.named_scope("greet"):
-        pl.semaphore_wait(barrier, greeted)
+        pl.semaphore_wait(barrier, len(near) + 2)
     for chunk in range(COUNT):
         send(0, chunk)
+    signal(ready.at[0], rounds[0])
     for n in (1, 2, 3, 4, 5):
         loads[n].start()
     loads[8].wait()
@@ -199,21 +209,21 @@
         size = PIECE_ROWS[chunk]
         at = PIECE_AT[chunk]
         core = cores[chunk]
-        for box, _ in boxes_order:
-            core[box] = jnp.dot(
-                states[LEVELS][chunk][order_ref[box]], cv[box], preferred_element_type=F32
-            ).astype(BF16)
-        for box, quarters in boxes_order:
-            rows = pl.ds(pl.multiple_of(box * LEAF, LEAF), LEAF)
-            made = jnp.dot(uv[rows, :], core[box].T, preferred_element_type=F32)
-            for quarter in range(4):
-                groups = [
-                    made[first : first + size]
-                    for first in range(quarter * PIECE, (quarter + 1) * PIECE, size)
-                ]
-                bx[box * 4 + quarter, at : at + size] = jnp.concatenate(groups, axis=1).astype(BF16)
-        with jax.named_scope("go"):
-            for box, quarters in boxes_order:
+        for part in (boxes_order,):
+            for box, _ in part:
+                core[box] = jnp.dot(
+                    states[LEVELS][chunk][order_ref[box]], cv[box], preferred_element_type=F32
+                ).astype(BF16)
+            for box, _ in part:
+                rows = pl.ds(pl.multiple_of(box * LEAF, LEAF), LEAF)
+                made = jnp.dot(uv[rows, :], core[box].T, preferred_element_type=F32)
+                for quarter in range(4):
+                    groups = [
+                        made[first : first + size]
+                        for first in range(quarter * PIECE, (quarter + 1) * PIECE, size)
+                    ]
+                    bx[box * 4 + quarter, at : at + size] = jnp.concatenate(groups, axis=1).astype(BF16)
+            for box, quarters in part:
                 for quarter, is_self in quarters:
                     if is_self:
                         own[chunk].start()
@@ -238,6 +248,14 @@
                 merge(level, chunk, first_pair(level, half) + n)
         elif kind == "s":
             send(*numbers)
+        elif kind == "h":
+            level_copy(*numbers).start()
+        elif kind == "r":
+            (n,) = numbers
+            with jax.named_scope(f"r{n}"):
+                pl.semaphore_wait(ready.at[n - 1], len(rounds[n - 1]))
+            if n < len(rounds):
+                signal(ready.at[n], rounds[n])
         else:
             need(4)
             need(5)
@@ -252,10 +270,7 @@
         pltpu.make_async_copy(rb.at[0], rb.at[0], own_sem.at[0]).wait()
         sent = bx.at[pl.ds(0, PEERS - 1)]
         pltpu.make_async_copy(sent, sent, far_send.at[0]).wait()
-        for level in range(LEVELS):
-            for chunk in range(COUNT):
-                moved = arrivals[level][chunk]
-                pltpu.make_async_copy(moved, moved, lev_send.at[level, chunk]).wait()
+        pltpu.make_async_copy(tv.at[0], tv.at[0], lev_send.at[0]).wait()
 
 
 def unpack(rb, out, ready, out_sem):
@@ -315,10 +330,11 @@
         + [
             pltpu.SemaphoreType.DMA((10,)),
             pltpu.SemaphoreType.DMA((1,)),
-            pltpu.SemaphoreType.DMA((LEVELS, COUNT)),
-            pltpu.SemaphoreType.DMA((LEVELS, COUNT, 2)),
+            pltpu.SemaphoreType.DMA((1,)),
+            pltpu.SemaphoreType.DMA((6 * COUNT,)),
             pltpu.SemaphoreType.DMA((1,)),
             pltpu.SemaphoreType.DMA((COUNT,)),
+            pltpu.SemaphoreType.REGULAR((3,)),
         ],
         compiler_params=pltpu.CompilerParams(
             collective_id=0, has_side_effects=True, vmem_limit_bytes=KERNEL_VMEM

time: 53.5 us -> 51.6 us (0.964)
  Pallas kernels: 53.4 us -> 51.5 us
    pallas_call x1, Pallas kernels: 52.2 us -> 50.3 us  [on_device(): call(vectors, leaf_basis, transfer.reshape(LEVELS, BOXES, 2 * RANK, RANK)...]
where the time goes in v3:
time: 51.6 us; the launch traced here: 51.5 us
  Pallas kernels  51.5 us (100%)
    pallas_call x1, Pallas kernels, on_device(): call(vectors, leaf_basis, transfer.reshape(LEVELS, BOXES, 2 * RANK, RANK)...  50.3 us
    pallas_call x1, Pallas kernels, on_device(): pl.pallas_call(unpack, out_shape=jax.ShapeDtypeStruct((BOXES * LEAF, COLS...  1.24 us

profile of v3, /device:TPU:1, one launch (start us, length us, event | category | flops | bytes accessed | tf_op | source)
XLA Modules:
  0.0 51.5 jit_solution(2628592895402929056)
XLA Ops:
  0.0 50.3 %butterfly.1.rb = bf16[32,128,128]{2,1,0:T(8,128)(2,1)S(1)} custom-call(bf16[2048,256]{1,0:T(8,128)(2,1)} %x_hbm.1, bf16[2048,256]{1,0:T(8,128)(2,1)} %v_hbm.1, bf16[4,8,512,256]{3,2,1,0:T(8,128)(2,1)} %bitcast.3, bf16[8,256,256]{2,1,0:T(8,128)(2,1)} %bitcast.4, bf16[2048,256]{1,0:T(8,128)(2,1)} %u_hbm.1, s32[8]{0:T(128)} %bitcast.5), custom_call_target="tpu_custom_call" | custom-call | tf_op jit(solution)/shard_map/butterfly/pallas_call | solution.py:344
  50.3 1.2 %unpack.1 = bf16[2048,256]{1,0:T(8,128)(2,1)} custom-call(bf16[32,128,128]{2,1,0:T(8,128)(2,1)S(1)} %butterfly.1.rb), custom_call_target="tpu_custom_call" | custom-call | tf_op jit(solution)/shard_map/unpack/pallas_call | solution.py:352

commit v4 on v3

--- a/solution.py
+++ b/solution.py
@@ -33,18 +33,18 @@
     ("m", 1, 0, 1), ("r", 2), ("m", 1, 1, 0), ("h", 2, 1, 0), ("m", 2, 0, 0), ("s", 3, 0),
     ("h", 2, 1, 1), ("m", 1, 1, 1), ("m", 2, 0, 1), ("m", 1, 2, 0), ("m", 2, 1, 0),
     ("s", 3, 1), ("h", 2, 2, 0), ("h", 2, 2, 1), ("m", 1, 2, 1), ("m", 1, 3, 0), ("r", 3),
-    ("m", 3, 0, 0), ("m", 3, 0, 1), ("f", 0), ("m", 1, 3, 1), ("m", 1, 4, 0), ("m", 1, 4, 1),
-    ("m", 2, 1, 1), ("m", 2, 2, 0), ("s", 3, 2), ("h", 2, 3, 0), ("h", 2, 3, 1),
-    ("h", 2, 4, 0), ("h", 2, 4, 1), ("m", 3, 1, 0), ("m", 3, 1, 1), ("f", 1), ("m", 2, 2, 1),
-    ("m", 3, 2, 0), ("m", 3, 2, 1), ("f", 2), ("m", 2, 3, 0), ("s", 3, 3), ("m", 2, 3, 1),
+    ("m", 3, 0, 0), ("m", 3, 0, 1), ("f", 0), ("m", 1, 3, 1), ("m", 1, 4, 0), ("m", 2, 1, 1),
+    ("m", 3, 1, 0), ("m", 3, 1, 1), ("m", 2, 2, 0), ("s", 3, 2), ("f", 1), ("h", 2, 3, 0),
+    ("h", 2, 3, 1), ("m", 1, 4, 1), ("m", 2, 2, 1), ("m", 2, 3, 0), ("s", 3, 3),
+    ("h", 2, 4, 0), ("h", 2, 4, 1), ("m", 3, 2, 0), ("m", 3, 2, 1), ("f", 2), ("m", 2, 3, 1),
     ("m", 2, 4, 0), ("s", 3, 4), ("m", 2, 4, 1), ("m", 3, 3, 0), ("m", 3, 3, 1), ("f", 3),
     ("m", 3, 4, 0), ("m", 3, 4, 1), ("f", 4),
 )
 
 
 def kernel(
-    x_hbm, v_hbm, t_hbm, c_hbm, u_hbm, order_ref, rb,
-    xv, vv, tv, cv, uv, bx, *rest,
+    x_hbm, v_hbm, t_hbm, c_hbm, u_hbm, order_hbm, rb,
+    xv, vv, tv, cv, uv, bx, order_ref, *rest,
 ):
     outer = lax.axis_index("outer")
     inner = lax.axis_index("inner")
@@ -98,10 +98,11 @@
                 (c_hbm, cv), (u_hbm, uv),
                 (x_hbm.at[sent_rows], xv.at[sent_rows]), (v_hbm.at[sent_rows], vv.at[sent_rows]),
                 (x_hbm.at[kept_rows], xv.at[kept_rows]), (v_hbm.at[kept_rows], vv.at[kept_rows]),
+                (order_hbm, order_ref),
             )
         )
     ]
-    for n in (6, 7):
+    for n in (6, 7, 8, 9):
         loads[n].start()
 
     barrier = pltpu.get_barrier_semaphore()
@@ -112,8 +113,10 @@
         return outer, x * 16 + z * 2 + lax.rem(inner + core_step, 2)
 
     near = [place(0, 0, 1), place(0, 1, 0), place(0, -1, 0), place(1, 0, 0)]
+    y_high, y = outer - lax.rem(outer, 4), lax.rem(outer, 4)
+    y_near = [(y_high + lax.rem(y + step, 4), inner) for step in (1, 3)]
     rounds = (
-        near,
+        [*near, partners[2]],
         [place(1, 0, 1), place(0, 2, 0), place(0, -2, 0)],
         [place(0, 0, 1), place(1, 0, 0), place(1, 0, 1)],
     )
@@ -122,7 +125,9 @@
         for device in devices:
             pl.semaphore_signal(semaphore, inc=1, device_id=device, device_id_type=MESH)
 
-    signal(barrier, [*near, *partners[2:]])
+    signal(barrier, [*near, *y_near])
+    for n in (0, 10):
+        loads[n].start()
 
     def first_pair(level, half):
         if level < LEVELS - 1:
@@ -158,8 +163,6 @@
     with jax.named_scope("load"):
         loads[6].wait()
         loads[7].wait()
-    for n in (8, 9, 0):
-        loads[n].start()
     for n in range(HALF):
         leaf((1 - flags[0]) * HALF + n)
     with jax.named_scope("greet"):
@@ -259,6 +262,7 @@
         else:
             need(4)
             need(5)
+            need(10)
             with jax.named_scope(f"f{numbers[0]}"):
                 finish(*numbers)
 
@@ -314,7 +318,7 @@
     call = pl.pallas_call(
         kernel,
         out_shape=pltpu.VMEM((PEERS, ALL_ROWS, LANES), BF16),
-        in_specs=[any_space] * 5 + [pl.BlockSpec(memory_space=pltpu.SMEM)],
+        in_specs=[any_space] * 6,
         out_specs=vmem,
         scratch_shapes=[
             pltpu.VMEM((BOXES * LEAF, COLS), BF16),
@@ -323,12 +327,13 @@
             pltpu.VMEM((BOXES, RANK, RANK), BF16),
             pltpu.VMEM((BOXES * LEAF, RANK), BF16),
             pltpu.VMEM((PEERS, ALL_ROWS, LANES), BF16),
+            pltpu.SMEM((BOXES,), jnp.int32),
         ]
         + [pltpu.VMEM((BOXES, width, RANK), BF16) for _, width in CHUNKS] * (LEVELS + 1)
         + [pltpu.VMEM((HALF, width, RANK), BF16) for _, width in CHUNKS] * LEVELS
         + [pltpu.VMEM((BOXES, width, RANK), BF16) for _, width in CHUNKS]
         + [
-            pltpu.SemaphoreType.DMA((10,)),
+            pltpu.SemaphoreType.DMA((11,)),
             pltpu.SemaphoreType.DMA((1,)),
             pltpu.SemaphoreType.DMA((1,)),
             pltpu.SemaphoreType.DMA((6 * COUNT,)),

time: 51.6 us -> 51 us (0.988)
  Pallas kernels: 51.5 us -> 50.9 us
    pallas_call x1, Pallas kernels: 50.3 us -> 49.7 us  [on_device(): call(vectors, leaf_basis, transfer.reshape(LEVELS, BOXES, 2 * RANK, RANK)...]
where the time goes in v4:
time: 51 us; the launch traced here: 50.9 us
  Pallas kernels  50.9 us (100%)
    pallas_call x1, Pallas kernels, on_device(): call(vectors, leaf_basis, transfer.reshape(LEVELS, BOXES, 2 * RANK, RANK)...  49.7 us
    pallas_call x1, Pallas kernels, on_device(): pl.pallas_call(unpack, out_shape=jax.ShapeDtypeStruct((BOXES * LEAF, COLS...  1.24 us

profile of v4, /device:TPU:1, one launch (start us, length us, event | category | flops | bytes accessed | tf_op | source)
XLA Modules:
  0.0 50.9 jit_solution(10631163997907150501)
XLA Ops:
  0.0 49.7 %butterfly.1.rb = bf16[32,128,128]{2,1,0:T(8,128)(2,1)S(1)} custom-call(bf16[2048,256]{1,0:T(8,128)(2,1)} %x_hbm.1, bf16[2048,256]{1,0:T(8,128)(2,1)} %v_hbm.1, bf16[4,8,512,256]{3,2,1,0:T(8,128)(2,1)} %bitcast.3, bf16[8,256,256]{2,1,0:T(8,128)(2,1)} %bitcast.4, bf16[2048,256]{1,0:T(8,128)(2,1)} %u_hbm.1, s32[8]{0:T(128)} %bitcast.5), custom_call_target="tpu_custom_call" | custom-call | tf_op jit(solution)/shard_map/butterfly/pallas_call | solution.py:349
  49.7 1.2 %unpack.1 = bf16[2048,256]{1,0:T(8,128)(2,1)} custom-call(bf16[32,128,128]{2,1,0:T(8,128)(2,1)S(1)} %butterfly.1.rb), custom_call_target="tpu_custom_call" | custom-call | tf_op jit(solution)/shard_map/unpack/pallas_call | solution.py:357

commit v5 on v4

--- a/solution.py
+++ b/solution.py
@@ -19,7 +19,7 @@
 CHUNKS = ((0, 32), (64, 64), (128, 64), (192, 64), (32, 32))
 COUNT = len(CHUNKS)
 LANES = 128
-KERNEL_VMEM = 65_600_000
+KERNEL_VMEM = 65_100_000
 PEERS = 32
 PIECE = BOXES * LEAF // PEERS
 PIECE_ROWS = tuple(PIECE * width // LANES for _, width in CHUNKS)
@@ -43,7 +43,7 @@
 
 
 def kernel(
-    x_hbm, v_hbm, t_hbm, c_hbm, u_hbm, order_hbm, rb,
+    x_hbm, v_hbm, t_hbm, c_hbm, u_hbm, order_hbm, rb, flat,
     xv, vv, tv, cv, uv, bx, order_ref, *rest,
 ):
     outer = lax.axis_index("outer")
@@ -270,46 +270,55 @@
         with jax.named_scope(f"far{chunk}"):
             arrived = rb.at[pl.ds(0, PEERS - 1), pl.ds(PIECE_AT[chunk], PIECE_ROWS[chunk])]
             pltpu.make_async_copy(arrived, arrived, far_recv.at[chunk]).wait()
+        if chunk == COUNT - 2:
+            pltpu.make_async_copy(rb.at[0], rb.at[0], own_sem.at[0]).wait()
+            for peer in range(PEERS):
+                lay_out(rb, flat, peer, LANES)
     with jax.named_scope("drain"):
-        pltpu.make_async_copy(rb.at[0], rb.at[0], own_sem.at[0]).wait()
         sent = bx.at[pl.ds(0, PEERS - 1)]
         pltpu.make_async_copy(sent, sent, far_send.at[0]).wait()
         pltpu.make_async_copy(tv.at[0], tv.at[0], lev_send.at[0]).wait()
 
 
-def unpack(rb, out, ready, out_sem):
+def lay_out(rb, target, peer, block):
+    step = min(PIECE_ROWS)
+    lane = lax.broadcasted_iota(jnp.int32, (step, LANES), 1)
+    for row in range(0, PIECE, step):
+        total = None
+        for chunk, (at, width) in enumerate(CHUNKS):
+            if not block <= at < block + LANES:
+                continue
+            group, inside = divmod(row, PIECE_ROWS[chunk])
+            first = PIECE_AT[chunk] + inside
+            part = rb[peer, first : first + step].astype(F32)
+            turn = (at - block - group * width) % LANES
+            part = pltpu.roll(part, turn, 1) if turn else part
+            mine = (lane >= at - block) & (lane < at - block + width)
+            total = part if total is None else jnp.where(mine, part, total)
+        base = peer * PIECE + row
+        target[base : base + step, :] = total.astype(BF16)
+
+
+def unpack(rb, flat, out, ready, out_sem):
     groups = 4
     peers = PEERS // groups
     rows = peers * PIECE
     outs = [
         pltpu.make_async_copy(
-            ready.at[pl.ds(g * rows, rows)], out.at[pl.ds(g * rows, rows)], out_sem.at[g]
+            ready.at[pl.ds(g * rows, rows)],
+            out.at[pl.ds(g * rows, rows), pl.ds(0, LANES)],
+            out_sem.at[g],
         )
         for g in range(groups)
     ]
-    step = min(PIECE_ROWS)
-    lane = lax.broadcasted_iota(jnp.int32, (step, LANES), 1)
+    outs.append(pltpu.make_async_copy(flat, out.at[:, pl.ds(LANES, LANES)], out_sem.at[groups]))
+    outs[groups].start()
     for g in range(groups):
         for peer in range(g * peers, (g + 1) * peers):
-            for block in range(0, COLS, LANES):
-                for row in range(0, PIECE, step):
-                    total = None
-                    for chunk, (at, width) in enumerate(CHUNKS):
-                        if not block <= at < block + LANES:
-                            continue
-                        group, inside = divmod(row, PIECE_ROWS[chunk])
-                        first = PIECE_AT[chunk] + inside
-                        part = rb[peer, first : first + step].astype(F32)
-                        turn = (at - block - group * width) % LANES
-                        part = pltpu.roll(part, turn, 1) if turn else part
-                        mine = (lane >= at - block) & (lane < at - block + width)
-                        total = part if total is None else jnp.where(mine, part, total)
-                    base = peer * PIECE + row
-                    ready[base : base + step, block : block + LANES] = total.astype(BF16)
+            lay_out(rb, ready, peer, 0)
         outs[g].start()
-    with jax.named_scope("outs"):
-        for copy in outs:
-            copy.wait()
+    for copy in outs:
+        copy.wait()
 
 
 def on_device(vectors, leaf_basis, transfer, core_mats, row_basis, box_order):
@@ -317,9 +326,12 @@
     vmem = pl.BlockSpec(memory_space=pltpu.VMEM)
     call = pl.pallas_call(
         kernel,
-        out_shape=pltpu.VMEM((PEERS, ALL_ROWS, LANES), BF16),
+        out_shape=(
+            pltpu.VMEM((PEERS, ALL_ROWS, LANES), BF16),
+            pltpu.VMEM((BOXES * LEAF, LANES), BF16),
+        ),
         in_specs=[any_space] * 6,
-        out_specs=vmem,
+        out_specs=(vmem, vmem),
         scratch_shapes=[
             pltpu.VMEM((BOXES * LEAF, COLS), BF16),
             pltpu.VMEM((BOXES * LEAF, RANK), BF16),
@@ -346,7 +358,7 @@
         ),
         name="butterfly",
     )
-    arrived = call(
+    arrived, flat = call(
         vectors,
         leaf_basis,
         transfer.reshape(LEVELS, BOXES, 2 * RANK, RANK),
@@ -357,12 +369,12 @@
     return pl.pallas_call(
         unpack,
         out_shape=jax.ShapeDtypeStruct((BOXES * LEAF, COLS), BF16),
-        in_specs=[vmem],
+        in_specs=[vmem, vmem],
         out_specs=any_space,
-        scratch_shapes=[pltpu.VMEM((BOXES * LEAF, COLS), BF16), pltpu.SemaphoreType.DMA((4,))],
+        scratch_shapes=[pltpu.VMEM((BOXES * LEAF, LANES), BF16), pltpu.SemaphoreType.DMA((5,))],
         compiler_params=pltpu.CompilerParams(vmem_limit_bytes=8 * 1024 * 1024),
         name="unpack",
-    )(arrived)
+    )(arrived, flat)
 
 
 def solution(mesh):

time: 51 us -> 50.8 us (level)
  no operation moved by 1% of the time
where the time goes in v5:
time: 50.8 us; the launch traced here: 50.7 us
  Pallas kernels  50.7 us (100%)
    pallas_call x1, Pallas kernels, on_device(): call(vectors, leaf_basis, transfer.reshape(LEVELS, BOXES, 2 * RANK, RANK)...  49.7 us
    pallas_call x1, Pallas kernels, on_device(): pl.pallas_call(unpack, out_shape=jax.ShapeDtypeStruct((BOXES * LEAF, COLS...  1.04 us

profile of v5, /device:TPU:1, one launch (start us, length us, event | category | flops | bytes accessed | tf_op | source)
XLA Modules:
  0.0 50.7 jit_solution(4321293897715551345)
XLA Ops:
  0.0 49.7 %butterfly.1 = (bf16[32,128,128]{2,1,0:T(8,128)(2,1)S(1)}, bf16[2048,128]{1,0:T(8,128)(2,1)S(1)}) custom-call(bf16[2048,256]{1,0:T(8,128)(2,1)} %x_hbm.1, bf16[2048,256]{1,0:T(8,128)(2,1)} %v_hbm.1, bf16[4,8,512,256]{3,2,1,0:T(8,128)(2,1)} %bitcast.3, bf16[8,256,256]{2,1,0:T(8,128)(2,1)} %bitcast.4, bf16[2048,256]{1,0:T(8,128)(2,1)} %u_hbm.1, s32[8]{0:T(128)} %bitcast.5), custom_call_target="tpu_custom_call" | custom-call | tf_op jit(solution)/shard_map/butterfly/pallas_call | solution.py:361
  49.7 1.0 %unpack.1 = bf16[2048,256]{1,0:T(8,128)(2,1)} custom-call(bf16[32,128,128]{2,1,0:T(8,128)(2,1)S(1)} %get-tuple-element.7.rb, bf16[2048,128]{1,0:T(8,128)(2,1)S(1)} %get-tuple-element.8.flat), custom_call_target="tpu_custom_call" | custom-call | tf_op jit(solution)/shard_map/unpack/pallas_call | solution.py:369
